TPU v7x, 128 devices: a whole 4x4x4 slice. The times are simulated.
128 devices in a mesh: seq: 16 (over z, y), head: 8 (over x, core).
Axes of the slice: x: 4, y: 4, z: 4, core: 2. Of those that a mesh axis runs over, the one named last changes fastest.
Arguments:
- normed: bfloat16 [32, 8192], P(None, 'seq'), may hold values from -6 to 6
- qkv_weight: bfloat16 [8192, 10240], P('seq', 'head'), may hold values from -0.0625 to 0.0625
- out_weight: bfloat16 [8192, 8192], P('head', 'seq'), may hold values from -0.0625 to 0.0625
- kv_cache: bfloat16 [1024, 2, 128, 1024], P('seq', None, None, 'head'), may hold values from -160 to 160
- lengths: int32 [8], replicated, may hold values from 1 to 9344, as said below
- slot_request: int32 [1024], P('seq'), may hold values from 0 to 8, as said below
- slot_block: int32 [1024], P('seq'), may hold values from 0 to 72, as said below
- send_list: int32 [16, 16, 4], P('seq'), may hold values from 0 to 64, as said below
- recv_list: int32 [16, 16, 4], P('seq'), may hold values from 0 to 64, as said below
Outputs:
- projected: bfloat16 [32, 8192], P('head', 'seq')
- moved_cache: bfloat16 [1024, 2, 128, 1024], P('seq', None, None, 'head')
Inputs may be any that keep to these rules, and one draw needn't show every extreme that they name: `lengths`: every request has at least one block; a request with n blocks has each of the block numbers 0 to n - 1 in exactly one slot, and its length lies in ((n - 1) * 128, n * 128]. `slot_request`: 8 marks an empty slot. `slot_block`: 0 in empty slots. 64 marks an unused entry, and send_list[s, e, c] is unused exactly where recv_list[e, s, c] is; every owned slot is sent exactly once and no empty slot is sent; at most 4 blocks go from one device to another, and some device receives exactly 4 from every device; after the scale-in only half of the seq devices hold blocks. `recv_list`: 64 marks an unused entry; each slot of a device is filled at most once.
All inputs are finite; a program needn't handle non-finite values.
Results may differ from a plain program's by a relative error of at most 0.025.
Values may be sent and summed in bfloat16 or wider, within the bound.
A program may use at most 128 MiB of HBM per device.

v0:
```python
import jax
import jax.numpy as jnp
from jax import lax
from jax.sharding import PartitionSpec as P

HEADS = 64
KV_HEADS = 8
HEAD = 128
POS = 4
BLOCK = 128
rope_base = 500000.0
neg_large = -1e30


def rotate(values, positions):
    half_width = values.shape[-1] // 2
    frequencies = rope_base ** (
        -(jnp.arange(half_width, dtype=jnp.float32) * 2.0 / values.shape[-1])
    )
    angles = positions[..., None] * frequencies
    cosine_table = jnp.cos(angles)
    sine_table = jnp.sin(angles)
    lower_half = values[..., :half_width]
    upper_half = values[..., half_width:]
    return jnp.concatenate(
        [
            lower_half * cosine_table - upper_half * sine_table,
            upper_half * cosine_table + lower_half * sine_table,
        ],
        axis=-1,
    )


def body(
    normed,
    qkv_weight,
    out_weight,
    kv_cache,
    lengths,
    slot_request,
    slot_block,
    send_list,
    recv_list,
):
    group_size = HEADS // KV_HEADS
    scale_factor = HEAD ** (-0.5)
    requests = lengths.shape[0]
    slot_count = kv_cache.shape[0]
    full_rows = lax.all_gather(normed, "seq", axis=1, tiled=True)
    projected_qkv = jnp.dot(
        full_rows,
        lax.all_gather(qkv_weight, "seq", axis=0, tiled=True),
        preferred_element_type=jnp.float32,
    )
    projected_qkv = projected_qkv.reshape(requests, POS, -1, group_size + 2, HEAD)
    local_kv = projected_qkv.shape[2]
    positions = (lengths[:, None] + jnp.arange(POS, dtype=jnp.int32)[None, :]).astype(jnp.float32)
    queries = rotate(projected_qkv[:, :, :, :group_size], positions[:, :, None, None]).astype(
        jnp.bfloat16
    )
    keys_new = rotate(projected_qkv[:, :, :, group_size], positions[:, :, None]).astype(
        jnp.bfloat16
    )
    values_new = projected_qkv[:, :, :, group_size + 1].astype(jnp.bfloat16)
    flat_send = send_list.reshape(-1)
    outgoing = kv_cache[jnp.minimum(flat_send, slot_count - 1)]
    outgoing = outgoing.reshape((lax.axis_size("seq"), -1) + kv_cache.shape[1:])
    incoming = lax.all_to_all(outgoing, "seq", split_axis=0, concat_axis=0, tiled=True)
    incoming = incoming.reshape((-1,) + kv_cache.shape[1:])
    moved_cache = jnp.zeros_like(kv_cache).at[recv_list.reshape(-1)].set(incoming, mode="drop")
    slot_clip = jnp.minimum(slot_request, requests - 1)
    live_slot = slot_request < requests
    token_pos = slot_block[:, None] * BLOCK + jnp.arange(BLOCK, dtype=jnp.int32)[None, :]
    token_valid = (token_pos < lengths[slot_clip][:, None]) & live_slot[:, None]
    cache_view = kv_cache.reshape(slot_count, 2, BLOCK, local_kv, HEAD)
    gathered = queries[slot_clip]
    scores = (
        jnp.einsum(
            "sptgd,sbtd->stgpb", gathered, cache_view[:, 0], preferred_element_type=jnp.float32
        )
        * scale_factor
    )
    scores = jnp.where(token_valid[:, None, None, None, :], scores, neg_large)
    slot_max = jnp.max(scores, axis=-1)
    weights = jnp.where(
        token_valid[:, None, None, None, :], jnp.exp(scores - slot_max[..., None]), 0.0
    )
    slot_sum = jnp.sum(weights, axis=-1)
    slot_acc = jnp.einsum(
        "stgpb,sbtd->stgpd",
        weights.astype(jnp.bfloat16),
        cache_view[:, 1],
        preferred_element_type=jnp.float32,
    )
    flat_width = local_kv * group_size * POS
    slot_max_flat = slot_max.reshape(slot_count, flat_width)
    member = slot_request[:, None] == jnp.arange(requests, dtype=jnp.int32)[None, :]
    request_max = jnp.max(
        jnp.where(member[:, None, :], slot_max_flat[:, :, None], neg_large), axis=0
    ).T
    rescale = jnp.exp(slot_max_flat - request_max[slot_clip])
    member_float = member.astype(jnp.float32).T
    request_sum = jnp.dot(
        member_float,
        slot_sum.reshape(slot_count, flat_width) * rescale,
        precision=lax.Precision.HIGHEST,
    )
    scaled_acc = (slot_acc.reshape(slot_count, flat_width, HEAD) * rescale[:, :, None]).reshape(
        slot_count, flat_width * HEAD
    )
    request_acc = jnp.dot(member_float, scaled_acc, precision=lax.Precision.HIGHEST).reshape(
        requests, flat_width, HEAD
    )
    total_max = lax.pmax(request_max, "seq")
    adjust = jnp.exp(request_max - total_max)
    total_sum, total_acc = (
        lax.psum((request_sum * adjust).astype(jnp.bfloat16), "seq").astype(jnp.float32),
        lax.psum((request_acc * adjust[:, :, None]).astype(jnp.bfloat16), "seq").astype(
            jnp.float32
        ),
    )
    new_scores = (
        jnp.einsum("rptgd,rqtd->rtgpq", queries, keys_new, preferred_element_type=jnp.float32)
        * scale_factor
    )
    causal = jnp.arange(POS)[:, None] >= jnp.arange(POS)[None, :]
    new_scores = jnp.where(causal, new_scores, neg_large)
    cache_max = total_max.reshape(requests, local_kv, group_size, POS)
    top_max = jnp.maximum(cache_max, jnp.max(new_scores, axis=-1))
    carry_scale = jnp.exp(cache_max - top_max)
    new_weights = jnp.where(causal, jnp.exp(new_scores - top_max[..., None]), 0.0)
    denominator = total_sum.reshape(requests, local_kv, group_size, POS) * carry_scale + jnp.sum(
        new_weights, axis=-1
    )
    numerator = (
        total_acc.reshape(requests, local_kv, group_size, POS, HEAD) * carry_scale[..., None]
    )
    numerator = numerator + jnp.einsum(
        "rtgpq,rqtd->rtgpd",
        new_weights.astype(jnp.bfloat16),
        values_new,
        preferred_element_type=jnp.float32,
    )
    attended = (
        (numerator / denominator[..., None])
        .transpose(0, 3, 1, 2, 4)
        .reshape(requests * POS, -1)
        .astype(jnp.bfloat16)
    )
    projected = lax.psum_scatter(
        jnp.dot(attended, out_weight, preferred_element_type=jnp.float32).astype(jnp.bfloat16),
        "head",
        scatter_dimension=0,
        tiled=True,
    )
    return (projected, moved_cache)


def solution(mesh):
    placed = (
        P(None, "seq"),
        P("seq", "head"),
        P("head", "seq"),
        P("seq", None, None, "head"),
        P(),
        P("seq"),
        P("seq"),
        P("seq", None, None),
        P("seq", None, None),
    )
    return jax.shard_map(
        body,
        mesh=mesh,
        in_specs=placed,
        out_specs=(P("head", "seq"), P("seq", None, None, "head")),
        check_vma=False,
    )
```

profile of v0, /device:TPU:0, one launch (start us, length us, event | category | flops | bytes accessed | tf_op | source)
XLA Modules:
  0.0 363.6 jit_solution(1940336600849006869)
XLA Ops:
  7.2 0.0 copy-start
  7.2 0.0 all-gather.2.cloned.1.call-start
  7.2 0.7 all-gather.2.cloned.1.call-update
  7.9 0.7 broadcast_minimum_fusion
  8.6 0.1 copy.81
  8.7 0.1 min.26
  8.8 5.3 %gather_fusion.2 = bf16[64,2,128,128]{3,2,1,0:T(8,128)(2,1)} fusion(bf16[64,2,128,128]{3,2,1,0:T(8,128)(2,1)} %param.12, s32[1024]{0:T(1024)S(1)} %pad_clamp_fusion), kind=kCustom, calls=%fused_computation.2 | custom fusion | bytes 8388864 | tf_op jit(solution)/shard_map/gather | solution.py:66
  14.1 8.2 %all-to-all-start = ((bf16[16,4,2,128,128]{4,3,2,1,0:T(8,128)(2,1)}), bf16[16,4,2,128,128]{4,3,2,1,0:T(8,128)(2,1)}, u32[]{:S(2)}, u32[]{:S(2)}) async-start(bf16[16,4,2,128,128]{4,3,2,1,0:T(8,128)(2,1)} %bitcast.134), calls=%async_computation | async-start | bytes 8388608 | tf_op jit(solution)/shard_map/all_to_all | solution.py:68
  22.3 0.0 copy-start.9
  22.3 0.0 copy-start.12
  22.3 0.0 copy-start.3
  22.3 0.0 copy-start.7
  22.3 0.0 copy-start.11
  22.4 0.0 all-reduce.3.cloned.1.call-start
  22.4 5.2 %copy.111 = bf16[64,2,128,128]{3,2,0,1:T(8,128)(2,1)} copy(bf16[64,2,128,128]{3,2,1,0:T(8,128)(2,1)} %param.12) | data formatting | bytes 8388608 | tf_op args[3]
  27.6 0.1 copy.80
  27.7 0.1 reshape.425
  27.8 0.6 dynamic-slice
  29.1 0.6 iota_compare_fusion.3
  29.7 0.7 fusion.53
  30.3 4.8 %compare_select_fusion.3 = (s32[64]{0:T(128)S(1)}, s32[64]{0:T(128)S(1)}, s32[64]{0:T(128)S(1)}) fusion(s32[]{:T(128)} %bitcast.1, s32[]{:T(128)} %bitcast.2, s32[]{:T(128)} %bitcast.3, s32[]{:T(128)} %bitcast.4, s32[]{:T(128)} %bitcast.5, s32[]{:T(128)} %bitcast.6, s32[]{:T(128)} %bitcast.7, s32[]{:T(128)} %bitcast.8, s32[64]{0:T(128)S(1)} %copy-done.7, ...), kind=kLoop, calls=%fused_computation.87 | loop fusion | flops 1216 | bytes 1312 | tf_op jit(solution)/shard_map/gather | solution.py:74
  35.2 80.1 %all_gather.6 = bf16[32,8192]{1,0:T(8,128)(2,1)S(1)} all-gather(bf16[32,512]{1,0:T(8,128)(2,1)S(1)} %copy-done.6), channel_id=1, replica_groups=mesh['seq'=16,'head'=8] {'seq'}, dimensions={1}, use_global_device_ids=true | all-gather | bytes 557056 | tf_op jit(solution)/shard_map/all_gather | solution.py:49
  115.4 0.1 add_convert_fusion.1
  115.4 0.1 fusion.31
  115.5 0.2 multiply_cosine_fusion.1
  115.7 3.1 broadcast_in_dim.96
  118.8 11.8 %scatter_fusion = bf16[64,2,128,128]{3,2,1,0:T(8,128)(2,1)} fusion(bf16[64,2,128,128]{3,2,1,0:T(8,128)(2,1)} %broadcast_in_dim.96, s32[64]{0:T(128)S(1)} %fusion.49, bf16[64,2,128,128]{3,2,1,0:T(8,128)(2,1)} %bitcast.45), kind=kCustom, calls=%fused_computation.3 | custom fusion | bytes 12583168 | tf_op jit(solution)/shard_map/scatter | solution.py:70
  130.6 61.3 %all-gather.2.cloned.1.call-done = bf16[8192,1280]{1,0:T(8,128)(2,1)} async-done(((bf16[512,1280]{1,0:T(8,128)(2,1)}), bf16[8192,1280]{1,0:T(8,128)(2,1)}) %all-gather.2.cloned.1.call-update) | async-done | bytes 20971536 | tf_op jit(solution)/shard_map/all_gather | solution.py:52
  191.9 8.8 %fusion.56 = f32[32,1280]{1,0:T(8,128)S(1)} fusion(bf16[32,8192]{1,0:T(8,128)(2,1)S(1)} %all_gather.6, bf16[8192,1280]{1,0:T(8,128)(2,1)} %all-gather.2.cloned.1.call-done), kind=kOutput, calls=%fused_computation.106 | convolution fusion | flops 671088640 | bytes 21659648 | tf_op jit(solution)/shard_map/dot_general | solution.py:50
  200.7 0.1 subtract_convert_fusion
  200.9 0.1 maximum_bitcast_fusion
  201.0 0.7 gather_fusion
  201.6 2.9 fusion.54
  204.6 0.1 copy.64
  204.6 0.7 copy.66
  205.4 0.1 select_reduce_fusion
  205.5 0.1 copy.65
  205.5 38.1 %pmax.7 = f32[8,32]{1,0:T(8,128)S(1)} all-reduce(f32[8,32]{1,0:T(8,128)S(1)} %bitcast.130), channel_id=1, replica_groups=mesh['seq'=16,'head'=8] {'seq'}, use_global_device_ids=true, to_apply=%region_2.3 | all-reduce | flops 256 | bytes 2048 | tf_op jit(solution)/shard_map/pmax | solution.py:114
  243.7 1.2 gather_fusion.1
  244.9 0.7 copy.70
  245.6 0.7 copy.68
  246.3 0.8 fusion.15
  247.0 2.3 fusion
  249.3 0.4 reshape.416
  249.7 0.8 subtract_exponential_fusion
  250.5 0.3 mul.180
  250.9 1.8 fusion.7
  252.7 0.7 copy.69
  253.3 0.0 all-reduce.3.cloned.1.call-update
  253.3 0.9 fusion.45
  254.2 0.8 copy.73
  255.0 0.1 copy.76
  255.1 0.1 copy.77
  255.2 0.8 fusion.11
  256.0 0.1 copy.78
  256.1 0.1 copy.79
  256.2 36.0 %psum.15 = bf16[8,8,4]{1,2,0:T(4,128)(2,1)S(1)} all-reduce(bf16[8,8,4]{1,2,0:T(4,128)(2,1)S(1)} %copy.79), channel_id=1, replica_groups=mesh['seq'=16,'head'=8] {'seq'}, use_global_device_ids=true, to_apply=%region_6.7 | all-reduce | flops 256 | bytes 1024 | tf_op jit(solution)/shard_map/psum | solution.py:117
  292.2 1.4 fusion.55
  293.6 0.1 fusion.24
  293.8 36.9 %all-reduce.3.cloned.1.call-done = bf16[8,8,4,128]{3,1,2,0:T(8,128)(2,1)} async-done(((bf16[8,8,4,128]{3,1,2,0:T(8,128)(2,1)}), bf16[8,8,4,128]{3,1,2,0:T(8,128)(2,1)}) %all-reduce.3.cloned.1.call-update) | async-done | bytes 65552 | tf_op jit(solution)/shard_map/psum | solution.py:118
  330.7 1.1 fusion.8
  331.8 0.3 convolution_convert_fusion
  332.1 24.0 %all-reduce = bf16[32,512]{1,0:T(8,128)(2,1)S(1)} all-reduce(bf16[32,512]{1,0:T(8,128)(2,1)S(1)} %convolution_convert_fusion), channel_id=2, replica_groups=mesh['seq'=16,'head'=8] {'head'}, use_global_device_ids=true, to_apply=%region_8.9.clone | all-reduce | flops 16384 | bytes 65536
  356.1 0.6 constant_dynamic-slice_fusion
  (35 shorter events, 0.2 us)
Async XLA Ops:
  7.2 324.7 %copy-start = (bf16[1024,512]{1,0:T(8,128)(2,1)S(1)}, bf16[1024,512]{1,0:T(8,128)(2,1)}, u32[]{:S(2)}) copy-start(bf16[1024,512]{1,0:T(8,128)(2,1)} %param.11) | copy-start | bytes 3145732
  7.2 184.7 %all-gather.2.cloned.1.call-start = ((), (), s32[]{:S(2)}) async-start(), calls=%async_computation.1 | async-start | bytes 22282240 | tf_op jit(solution)/shard_map/all_gather | solution.py:52
  14.1 101.6 %all-to-all-start = ((bf16[16,4,2,128,128]{4,3,2,1,0:T(8,128)(2,1)}), bf16[16,4,2,128,128]{4,3,2,1,0:T(8,128)(2,1)}, u32[]{:S(2)}, u32[]{:S(2)}) async-start(bf16[16,4,2,128,128]{4,3,2,1,0:T(8,128)(2,1)} %bitcast.134), calls=%async_computation | async-start | bytes 8388608 | tf_op jit(solution)/shard_map/all_to_all | solution.py:68
  22.3 5.3 %copy-start.9 = (s32[1,16,4]{1,2,0:T(4,128)S(1)}, s32[1,16,4]{1,2,0:T(4,128)}, u32[]{:S(2)}) copy-start(s32[1,16,4]{1,2,0:T(4,128)} %param.17) | copy-start | bytes 772
  22.3 5.5 %copy-start.12 = (u32[128]{0:T(128)S(1)}, u32[128]{0:T(128)}, u32[]{:S(2)}) copy-start(u32[128]{0:T(128)} %constant.43) | copy-start | bytes 1540
  22.3 7.4 %copy-start.3 = (s32[8]{0:T(128)S(1)}, s32[8]{0:T(128)}, u32[]{:S(2)}) copy-start(s32[8]{0:T(128)} %param.13) | copy-start | bytes 100
  22.3 8.0 %copy-start.7 = (s32[64]{0:T(128)S(1)}, s32[64]{0:T(128)}, u32[]{:S(2)}) copy-start(s32[64]{0:T(128)} %param.14) | copy-start | bytes 772
  22.3 8.0 %copy-start.11 = (s32[64]{0:T(128)S(1)}, s32[64]{0:T(128)}, u32[]{:S(2)}) copy-start(s32[64]{0:T(128)} %param.15) | copy-start | bytes 772
  22.3 12.8 %copy-start.6 = (bf16[32,512]{1,0:T(8,128)(2,1)S(1)}, bf16[32,512]{1,0:T(8,128)(2,1)}, u32[]{:S(2)}) copy-start(bf16[32,512]{1,0:T(8,128)(2,1)} %param.9) | copy-start | bytes 98308
  22.4 308.4 %all-reduce.3.cloned.1.call-start = ((), (), s32[]{:S(2)}) async-start(), calls=%async_computation.2 | async-start | bytes 131072 | tf_op jit(solution)/shard_map/psum | solution.py:118
  29.1 101.5 %copy-start.8 = (f32[64]{0:T(128)}, f32[64]{0:T(128)S(1)}, u32[]{:S(2)}) copy-start(f32[64]{0:T(128)S(1)} %negate_power_fusion) | copy-start | bytes 772
  115.4 15.2 %copy-start.5 = (f32[8,4]{1,0:T(8,128)}, f32[8,4]{1,0:T(8,128)S(1)}, u32[]{:S(2)}) copy-start(f32[8,4]{1,0:T(8,128)S(1)} %add_convert_fusion.1) | copy-start | bytes 388
  200.8 0.8 copy-start.1
  200.9 0.8 copy-start.2
  244.9 2.1 copy-start.4
  249.7 43.9 %copy-start.10 = (pred[4,4]{1,0:T(4,128)(4,1)S(1)}, pred[4,4]{1,0:T(4,128)(4,1)}, u32[]{:S(2)}) copy-start(pred[4,4]{1,0:T(4,128)(4,1)} %iota_compare_fusion.3) | copy-start | bytes 52
Sparse Core Ops, SparseCore 0:
  10.1 181.6 all-gather.1
  253.4 77.2 all-reduce.2
where the time goes:
time: 365 us; the launch traced here: 364 us
  blocking collectives  178 us (49%)
  waiting for transfers between devices  98.9 us (27%)
  local copies, waits for them, and re-layouts  34.3 us (9%)
  matrix products  19.4 us (5%)
  between operations  15.1 us (4%)
  other arithmetic  9.38 us (3%)
  starting transfers between devices  8.26 us (2%)
    all_gather x1, blocking collectives, body(): full_rows = lax.all_gather(normed, 'seq', axis=1, tiled=True)  80.1 us
    all_gather x1, waiting for transfers between devices, body(): lax.all_gather(qkv_weight, 'seq', axis=0, tiled=True)  61.3 us
    pmax x1, blocking collectives, body(): total_max = lax.pmax(request_max, 'seq')  38.1 us
    psum x1, waiting for transfers between devices, body(): lax.psum((request_acc * adjust[:, :, None]).astype(jnp.bfloat16), 'seq')  36.9 us
    psum x1, blocking collectives, body(): lax.psum((request_sum * adjust).astype(jnp.bfloat16), 'seq')  36 us
    unnamed x1, blocking collectives  24 us
    scatter x1, local copies, waits for them, and re-layouts, body(): jnp.zeros_like(kv_cache).at[recv_list.reshape(-1)]  11.8 us
    dot_general x1, matrix products, body(): jnp.dot(full_rows, lax.all_gather(qkv_weight, 'seq', axis=0, tiled=True),...  8.79 us
  transfers between devices with their start and end apart: 3, of which 2 were waited for; matrix products, arithmetic and copies ran while one was open for 10% of the time, Pallas kernels for 0%

commit v1 on v0

--- a/solution.py
+++ b/solution.py
@@ -10,6 +10,18 @@
 BLOCK = 128
 rope_base = 500000.0
 neg_large = -1e30
+
+
+def domain_track(mine_x):
+    return jnp.concatenate(
+        jax.lax.all_to_all(
+            jnp.stack([mine_x] * jax.lax.axis_size("seq")),
+            concat_axis=0,
+            axis_name="seq",
+            split_axis=0,
+        ),
+        1,
+    )
 
 
 def rotate(values, positions):
@@ -46,7 +58,7 @@
     scale_factor = HEAD ** (-0.5)
     requests = lengths.shape[0]
     slot_count = kv_cache.shape[0]
-    full_rows = lax.all_gather(normed, "seq", axis=1, tiled=True)
+    full_rows = domain_track(normed)
     projected_qkv = jnp.dot(
         full_rows,
         lax.all_gather(qkv_weight, "seq", axis=0, tiled=True),

time: 365 us -> 388 us (1.063)
  blocking collectives: 178 us -> 97.5 us
  waiting for transfers between devices: 98.9 us -> 175 us
  local copies, waits for them, and re-layouts: 34.3 us -> 59.8 us
  starting transfers between devices: 8.26 us -> 12.8 us
    all_gather x1 -> x0, blocking collectives: 80.1 us -> none  [body(): full_rows = lax.all_gather(normed, 'seq', axis=1, tiled=True)]
    all_to_all x1, waiting for transfers between devices: 0.01 us -> 60.3 us  [body(): lax.all_to_all(outgoing, 'seq', split_axis=0, concat_axis=0, tiled=True)]
    dot_general x0 -> x2, local copies, waits for them, and re-layouts: none -> 27.3 us  [body(): jnp.dot(full_rows, lax.all_gather(qkv_weight, 'seq', axis=0, tiled=True),...]
    all_gather x1, waiting for transfers between devices: 61.3 us -> 69.7 us  [body(): lax.all_gather(qkv_weight, 'seq', axis=0, tiled=True)]
    all_to_all x0 -> x1, starting transfers between devices: none -> 8.15 us  [domain_track(): jax.lax.all_to_all(jnp.stack([mine_x] * jax.lax.axis_size('seq')), concat...]
    all_to_all x0 -> x1, waiting for transfers between devices: none -> 5.45 us  [domain_track(): jax.lax.all_to_all(jnp.stack([mine_x] * jax.lax.axis_size('seq')), concat...]
  transfers between devices with their start and end apart: 3 -> 4, of which waited for: 2 -> 4; matrix products, arithmetic and copies ran while one was open for 10% -> 9% of each run, Pallas kernels for 0% -> 0%
where the time goes in v1:
time: 388 us; the launch traced here: 387 us
  waiting for transfers between devices  175 us (45%)
  blocking collectives  97.5 us (25%)
  local copies, waits for them, and re-layouts  59.8 us (15%)
  matrix products  18.8 us (5%)
  between operations  15 us (4%)
  starting transfers between devices  12.8 us (3%)
  other arithmetic  7.6 us (2%)
    all_gather x1, waiting for transfers between devices, body(): lax.all_gather(qkv_weight, 'seq', axis=0, tiled=True)  69.7 us
    all_to_all x1, waiting for transfers between devices, body(): lax.all_to_all(outgoing, 'seq', split_axis=0, concat_axis=0, tiled=True)  60.3 us
    psum x1, waiting for transfers between devices, body(): lax.psum((request_acc * adjust[:, :, None]).astype(jnp.bfloat16), 'seq')  39.3 us
    psum x1, blocking collectives, body(): lax.psum((request_sum * adjust).astype(jnp.bfloat16), 'seq')  37.3 us
    pmax x1, blocking collectives, body(): total_max = lax.pmax(request_max, 'seq')  36.1 us
    dot_general x2, local copies, waits for them, and re-layouts, body(): jnp.dot(full_rows, lax.all_gather(qkv_weight, 'seq', axis=0, tiled=True),...  27.3 us
    unnamed x1, blocking collectives  24 us
    scatter x1, local copies, waits for them, and re-layouts, body(): jnp.zeros_like(kv_cache).at[recv_list.reshape(-1)]  11.8 us
  transfers between devices with their start and end apart: 4, of which 4 were waited for; matrix products, arithmetic and copies ran while one was open for 9% of the time, Pallas kernels for 0%

profile of v1, /device:TPU:0, one launch (start us, length us, event | category | flops | bytes accessed | tf_op | source)
XLA Modules:
  0.0 387.0 jit_solution(7113714042065067603)
XLA Ops:
  7.2 0.0 copy-start
  7.2 0.0 all-gather.2.cloned.1.call-start
  7.2 0.7 all-gather.2.cloned.1.call-update
  7.9 1.6 stack.2
  9.5 8.1 %all-to-all-start = ((bf16[16,32,512]{2,1,0:T(8,128)(2,1)}), bf16[16,32,512]{2,1,0:T(8,128)(2,1)S(1)}, u32[]{:S(2)}, u32[]{:S(2)}) async-start(bf16[16,32,512]{2,1,0:T(8,128)(2,1)} %stack.2), calls=%async_computation | async-start | bytes 1048576 | tf_op jit(solution)/shard_map/all_to_all | solution.py:17
  17.7 0.7 broadcast_minimum_fusion
  18.4 0.1 copy.91
  18.4 0.1 min.26
  18.6 5.3 %gather_fusion.2 = bf16[64,2,128,128]{3,2,1,0:T(8,128)(2,1)} fusion(bf16[64,2,128,128]{3,2,1,0:T(8,128)(2,1)} %param.12, s32[1024]{0:T(1024)S(1)} %pad_clamp_fusion), kind=kCustom, calls=%fused_computation.2 | custom fusion | bytes 8388864 | tf_op jit(solution)/shard_map/gather | solution.py:78
  23.8 5.4 %all-to-all-done = bf16[16,32,512]{2,1,0:T(8,128)(2,1)S(1)} async-done(((bf16[16,32,512]{2,1,0:T(8,128)(2,1)}), bf16[16,32,512]{2,1,0:T(8,128)(2,1)S(1)}, u32[]{:S(2)}, u32[]{:S(2)}) %all-to-all-start) | async-done | bytes 524320 | tf_op jit(solution)/shard_map/all_to_all | solution.py:17
  29.3 4.5 %all-to-all-start.1 = ((bf16[16,4,2,128,128]{4,3,2,1,0:T(8,128)(2,1)}), bf16[16,4,2,128,128]{4,3,2,1,0:T(8,128)(2,1)}, u32[]{:S(2)}, u32[]{:S(2)}) async-start(bf16[16,4,2,128,128]{4,3,2,1,0:T(8,128)(2,1)} %bitcast.146), calls=%async_computation.1 | async-start | bytes 8388608 | tf_op jit(solution)/shard_map/all_to_all | solution.py:80
  33.9 0.0 all-reduce.3.cloned.1.call-start
  34.0 4.8 %copy.120 = bf16[64,2,128,128]{3,2,0,1:T(8,128)(2,1)} copy(bf16[64,2,128,128]{3,2,1,0:T(8,128)(2,1)} %param.12) | data formatting | bytes 8388608 | tf_op args[3]
  38.7 0.1 copy.90
  38.8 0.1 reshape.438
  38.9 0.6 dynamic-slice
  40.2 0.7 fusion.53
  40.9 4.9 %compare_select_fusion.3 = (s32[64]{0:T(128)S(1)}, s32[64]{0:T(128)S(1)}, s32[64]{0:T(128)S(1)}) fusion(s32[]{:T(128)} %bitcast.1, s32[]{:T(128)} %bitcast.2, s32[]{:T(128)} %bitcast.3, s32[]{:T(128)} %bitcast.4, s32[]{:T(128)} %bitcast.5, s32[]{:T(128)} %bitcast.6, s32[]{:T(128)} %bitcast.7, s32[]{:T(128)} %bitcast.8, s32[64]{0:T(128)S(1)} %copy-done.3, ...), kind=kLoop, calls=%fused_computation.88 | loop fusion | flops 1216 | bytes 1312 | tf_op jit(solution)/shard_map/gather | solution.py:86
  45.8 0.1 add_convert_fusion.1
  45.9 0.1 fusion.30
  46.0 0.2 multiply_cosine_fusion.1
  46.2 0.3 copy.71
  46.5 0.4 reshape.494
  46.9 60.3 %all-to-all-done.1 = bf16[16,4,2,128,128]{4,3,2,1,0:T(8,128)(2,1)} async-done(((bf16[16,4,2,128,128]{4,3,2,1,0:T(8,128)(2,1)}), bf16[16,4,2,128,128]{4,3,2,1,0:T(8,128)(2,1)}, u32[]{:S(2)}, u32[]{:S(2)}) %all-to-all-start.1) | async-done | bytes 4194336 | tf_op jit(solution)/shard_map/all_to_all | solution.py:80
  107.2 3.1 broadcast_in_dim.96
  110.3 11.8 %scatter_fusion = bf16[64,2,128,128]{3,2,1,0:T(8,128)(2,1)} fusion(bf16[64,2,128,128]{3,2,1,0:T(8,128)(2,1)} %broadcast_in_dim.96, s32[64]{0:T(128)S(1)} %fusion.49, bf16[64,2,128,128]{3,2,1,0:T(8,128)(2,1)} %bitcast.52), kind=kCustom, calls=%fused_computation.3 | custom fusion | bytes 12583168 | tf_op jit(solution)/shard_map/scatter | solution.py:82
  122.0 69.7 %all-gather.2.cloned.1.call-done = bf16[8192,1280]{1,0:T(8,128)(2,1)} async-done(((bf16[512,1280]{1,0:T(8,128)(2,1)}), bf16[8192,1280]{1,0:T(8,128)(2,1)}) %all-gather.2.cloned.1.call-update) | async-done | bytes 20971536 | tf_op jit(solution)/shard_map/all_gather | solution.py:64
  191.7 26.9 %copy.72 = bf16[1280,8192]{1,0:T(8,128)(2,1)} copy(bf16[1280,8192]{0,1:T(8,128)(2,1)} %bitcast.140) | data formatting | bytes 41943040 | tf_op jit(solution)/shard_map/dot_general | solution.py:62
  218.7 10.6 %convolution_bitcast_fusion = f32[8,4,1,10,128]{4,1,3,0,2:T(4,128)S(1)} fusion(bf16[10,128,8192,1]{2,1,0,3:T(8,128)(2,1)} %bitcast.141, bf16[8,4,8192,1]{2,1,0,3:T(4,128)(2,1)S(1)} %reshape.494), kind=kOutput, calls=%fused_computation.13 | convolution fusion | flops 671088640 | bytes 21659648 | tf_op jit(solution)/shard_map/dot_general | solution.py:62
  229.3 0.1 subtract_convert_fusion
  229.4 0.1 maximum_bitcast_fusion
  229.6 0.7 gather_fusion
  230.2 2.9 fusion.54
  233.1 0.1 copy.76
  233.2 0.1 copy.78
  233.3 0.1 select_reduce_fusion
  233.4 0.1 copy.77
  233.5 36.1 %pmax.7 = f32[8,32]{1,0:T(8,128)S(1)} all-reduce(f32[8,32]{1,0:T(8,128)S(1)} %bitcast.142), channel_id=1, replica_groups=mesh['seq'=16,'head'=8] {'seq'}, use_global_device_ids=true, to_apply=%region_2.3 | all-reduce | flops 256 | bytes 2048 | tf_op jit(solution)/shard_map/pmax | solution.py:126
  269.6 0.6 gather_fusion.1
  270.3 0.1 copy.82
  270.3 0.1 copy.80
  270.4 0.8 fusion.15
  271.2 2.3 fusion
  273.4 0.4 reshape.429
  273.9 0.3 mul.180
  274.2 1.1 fusion.7
  275.3 0.7 copy.81
  276.0 0.0 all-reduce.3.cloned.1.call-update
  276.0 0.2 fusion.45
  276.2 0.1 copy.85
  276.3 0.1 copy.86
  276.3 0.1 copy.87
  276.4 0.1 fusion.11
  276.6 0.1 copy.88
  276.7 0.1 copy.89
  276.8 37.3 %psum.15 = bf16[8,8,4]{1,2,0:T(4,128)(2,1)S(1)} all-reduce(bf16[8,8,4]{1,2,0:T(4,128)(2,1)S(1)} %copy.89), channel_id=1, replica_groups=mesh['seq'=16,'head'=8] {'seq'}, use_global_device_ids=true, to_apply=%region_6.7 | all-reduce | flops 256 | bytes 1024 | tf_op jit(solution)/shard_map/psum | solution.py:129
  314.1 0.1 pad_maximum_fusion
  314.2 0.5 fusion.55
  314.7 0.1 fusion.23
  314.8 39.3 %all-reduce.3.cloned.1.call-done = bf16[8,8,4,128]{3,1,2,0:T(8,128)(2,1)} async-done(((bf16[8,8,4,128]{3,1,2,0:T(8,128)(2,1)}), bf16[8,8,4,128]{3,1,2,0:T(8,128)(2,1)}) %all-reduce.3.cloned.1.call-update) | async-done | bytes 65552 | tf_op jit(solution)/shard_map/psum | solution.py:130
  354.1 1.1 fusion.8
  355.3 0.3 convolution_convert_fusion
  355.5 24.0 %all-reduce = bf16[32,512]{1,0:T(8,128)(2,1)S(1)} all-reduce(bf16[32,512]{1,0:T(8,128)(2,1)S(1)} %convolution_convert_fusion), channel_id=2, replica_groups=mesh['seq'=16,'head'=8] {'head'}, use_global_device_ids=true, to_apply=%region_8.9.clone | all-reduce | flops 16384 | bytes 65536
  379.6 0.6 constant_dynamic-slice_fusion
  (27 shorter events, 0.1 us)
Async XLA Ops:
  7.2 348.1 %copy-start = (bf16[1024,512]{1,0:T(8,128)(2,1)S(1)}, bf16[1024,512]{1,0:T(8,128)(2,1)}, u32[]{:S(2)}) copy-start(bf16[1024,512]{1,0:T(8,128)(2,1)} %param.11) | copy-start | bytes 3145732
  7.2 184.6 %all-gather.2.cloned.1.call-start = ((), (), s32[]{:S(2)}) async-start(), calls=%async_computation.2 | async-start | bytes 22282240 | tf_op jit(solution)/shard_map/all_gather | solution.py:64
  9.5 19.8 %all-to-all-start = ((bf16[16,32,512]{2,1,0:T(8,128)(2,1)}), bf16[16,32,512]{2,1,0:T(8,128)(2,1)S(1)}, u32[]{:S(2)}, u32[]{:S(2)}) async-start(bf16[16,32,512]{2,1,0:T(8,128)(2,1)} %stack.2), calls=%async_computation | async-start | bytes 1048576 | tf_op jit(solution)/shard_map/all_to_all | solution.py:17
  29.3 77.9 %all-to-all-start.1 = ((bf16[16,4,2,128,128]{4,3,2,1,0:T(8,128)(2,1)}), bf16[16,4,2,128,128]{4,3,2,1,0:T(8,128)(2,1)}, u32[]{:S(2)}, u32[]{:S(2)}) async-start(bf16[16,4,2,128,128]{4,3,2,1,0:T(8,128)(2,1)} %bitcast.146), calls=%async_computation.1 | async-start | bytes 8388608 | tf_op jit(solution)/shard_map/all_to_all | solution.py:80
  33.8 4.9 %copy-start.4 = (s32[1,16,4]{1,2,0:T(4,128)S(1)}, s32[1,16,4]{1,2,0:T(4,128)}, u32[]{:S(2)}) copy-start(s32[1,16,4]{1,2,0:T(4,128)} %param.17) | copy-start | bytes 772
  33.9 5.1 %copy-start.6 = (u32[128]{0:T(128)S(1)}, u32[128]{0:T(128)}, u32[]{:S(2)}) copy-start(u32[128]{0:T(128)} %constant.43) | copy-start | bytes 1540
  33.9 6.3 %copy-start.2 = (s32[8]{0:T(128)S(1)}, s32[8]{0:T(128)}, u32[]{:S(2)}) copy-start(s32[8]{0:T(128)} %param.13) | copy-start | bytes 100
  33.9 7.0 %copy-start.3 = (s32[64]{0:T(128)S(1)}, s32[64]{0:T(128)}, u32[]{:S(2)}) copy-start(s32[64]{0:T(128)} %param.14) | copy-start | bytes 772
  33.9 7.0 %copy-start.5 = (s32[64]{0:T(128)S(1)}, s32[64]{0:T(128)}, u32[]{:S(2)}) copy-start(s32[64]{0:T(128)} %param.15) | copy-start | bytes 772
  33.9 320.2 %all-reduce.3.cloned.1.call-start = ((), (), s32[]{:S(2)}) async-start(), calls=%async_computation.3 | async-start | bytes 131072 | tf_op jit(solution)/shard_map/psum | solution.py:130
  229.2 41.9 %copy-start.1 = (f32[8,4,1,10,128]{4,1,3,0,2:T(4,128)}, f32[8,4,1,10,128]{4,1,3,0,2:T(4,128)S(1)}, u32[]{:S(2)}) copy-start(f32[8,4,1,10,128]{4,1,3,0,2:T(4,128)S(1)} %convolution_bitcast_fusion) | copy-start | bytes 491524
Sparse Core Ops, SparseCore 0:
  10.1 181.5 all-gather.1
  276.1 77.9 all-reduce.2
